TPU v7x, 32 devices: a whole 2x2x4 slice. The times are simulated.
32 devices in a mesh: tm: 2 (over y), space: 16 (over z, x, core).
Axes of the slice: x: 2, y: 2, z: 4, core: 2. Of those that a mesh axis runs over, the one named last changes fastest.
Arguments:
- slice_starts: float32 [2, 2, 256, 256], P('tm', None, 'space'), may hold values from 0.2 to 1.5
- habitat: int32 [256, 256], P('space'), may hold values from 0 to 7
- capacity_table: float32 [8], replicated, may hold values from 0.5 to 3
- prey_motility: float32 [8], replicated, may hold values from 0.03 to 0.2
- predator_motility: float32 [8], replicated, may hold values from 0.03 to 0.2
Outputs:
- slice_ends: float32 [2, 2, 256, 256], P('tm', None, 'space')
All inputs are finite; a program needn't handle non-finite values.
Results may differ from a plain program's by a relative error of at most 0.00002.
Values sent between devices are 32-bit elements; how exact they have to be, the bound alone decides.
No kernel may reach another device: no remote copies, remote signals or barrier semaphores. Data moves between devices by JAX's collectives and lax.ppermute only.
A program may use at most 64 MiB of HBM per device.

v0:
```python
import jax
import jax.numpy as jnp
from jax import lax
from jax.sharding import PartitionSpec as P

GROWTH = 0.5
ATTACK = 0.5
HANDLING = 1.0
CONVERSION = 0.6
MORTALITY = 0.3
TAXIS = 0.15


def with_halo(cells, sides, width):
    for axis, dim in sides:
        count = lax.axis_size(axis)
        head = lax.slice_in_dim(cells, 0, width, axis=dim)
        tail = lax.slice_in_dim(cells, cells.shape[dim] - width, cells.shape[dim], axis=dim)
        cells = jnp.concatenate(
            [
                lax.ppermute(tail, axis, [(i, (i + 1) % count) for i in range(count)]),
                cells,
                lax.ppermute(head, axis, [((i + 1) % count, i) for i in range(count)]),
            ],
            axis=dim,
        )
    return cells


def from_behind(array, axis, by):
    peers = lax.axis_size(axis)
    pairs = [(i, i + by) for i in range(peers) if 0 <= i + by < peers]
    return lax.ppermute(array, axis, pairs)


def laplace(field):
    inner = field[1:-1]
    return field[2:] + field[:-2] + jnp.roll(inner, 1, -1) + jnp.roll(inner, -1, -1) - 4.0 * inner


def advance(prey, predator, prey_mob, pred_mob, capacity, step_dt, inv_h2):
    spread_prey = laplace(prey_mob * prey) * inv_h2
    spread_pred = laplace(pred_mob * predator) * inv_h2
    row_flux = 0.5 * (predator[1:] + predator[:-1]) * (prey[1:] - prey[:-1])
    inner_prey = prey[1:-1]
    inner_pred = predator[1:-1]
    col_flux = (
        0.5
        * (inner_pred + jnp.roll(inner_pred, -1, -1))
        * (jnp.roll(inner_prey, -1, -1) - inner_prey)
    )
    taxis_div = (row_flux[1:] - row_flux[:-1] + col_flux - jnp.roll(col_flux, 1, -1)) * inv_h2
    response = inner_prey * inner_pred / (1.0 + HANDLING * jnp.abs(inner_prey))
    new_prey = inner_prey + step_dt * (
        spread_prey + GROWTH * inner_prey * (1.0 - inner_prey / capacity) - ATTACK * response
    )
    new_pred = inner_pred + step_dt * (
        spread_pred - TAXIS * taxis_div + CONVERSION * ATTACK * response - MORTALITY * inner_pred
    )
    return jnp.stack([new_prey, new_pred])


def restrict(field):
    shape = field.shape
    blocks = field.reshape(shape[:-2] + (shape[-2] // 2, 2, shape[-1] // 2, 2))
    return (
        blocks[..., 0, :, 0] + blocks[..., 0, :, 1] + blocks[..., 1, :, 0] + blocks[..., 1, :, 1]
    ) * 0.25


def prolong(field):
    return jnp.repeat(jnp.repeat(field, 2, axis=-2), 2, axis=-1)


def lookup(table, habitat):
    result = jnp.zeros(habitat.shape, jnp.float32)
    for klass in range(table.shape[0]):
        result = jnp.where(habitat == klass, table[klass], result)
    return result


def coarse_step(coarse_state, coarse_coef):
    widened = with_halo(coarse_state, (("space", 1),), 1)
    return advance(
        widened[0], widened[1], coarse_coef[0], coarse_coef[1], coarse_coef[2, 1:-1], 2.0, 0.25
    )


def on_device(slice_starts, habitat, capacity_table, prey_motility, predator_motility):
    start = slice_starts[0]
    coefficients = jnp.stack(
        [
            lookup(prey_motility, habitat),
            lookup(predator_motility, habitat),
            lookup(capacity_table, habitat),
        ]
    )
    coef_wide = with_halo(coefficients, (("space", 1),), 2)
    coarse_coef = restrict(coef_wide)
    fine_state = start
    for sweep in range(2):
        widened = with_halo(fine_state, (("space", 1),), 1)
        fine_state = advance(
            widened[0],
            widened[1],
            coef_wide[0, 1:-1],
            coef_wide[1, 1:-1],
            coef_wide[2, 2:-2],
            1.0,
            1.0,
        )
    correction = fine_state - prolong(coarse_step(restrict(start), coarse_coef))
    my_slice = lax.axis_index("tm")
    slice_count = lax.axis_size("tm")
    current = start
    own_coarse = jnp.zeros_like(restrict(start))
    for handoff in range(slice_count):
        coarse_next = coarse_step(restrict(current), coarse_coef)
        own_coarse = jnp.where(my_slice == handoff, coarse_next, own_coarse)
        if handoff + 1 < slice_count:
            result = prolong(coarse_next) + correction
            arrived = from_behind(result, "tm", 1)
            current = jnp.where(my_slice == handoff + 1, arrived, current)
    slice_result = prolong(own_coarse) + correction
    return slice_result[None]


def solution(mesh):
    placed = (P("tm", None, "space", None), P("space", None), P(), P(), P())
    return jax.shard_map(
        on_device,
        mesh=mesh,
        in_specs=placed,
        out_specs=P("tm", None, "space", None),
        check_vma=False,
    )
```

profile of v0, /device:TPU:0, one launch (start us, length us, event | category | flops | bytes accessed | tf_op | source)
XLA Modules:
  0.0 85.7 jit_solution(11796769566358413670)
XLA Ops:
  0.0 1.6 %fusion.153 = (f32[1]{0:T(128)}, f32[1]{0:T(128)}, f32[1]{0:T(128)}, f32[1]{0:T(128)}, f32[1]{0:T(128)}, /*index=5*/f32[1]{0:T(128)}, f32[1]{0:T(128)}, f32[1]{0:T(128)}) fusion(f32[8]{0:T(128)} %param.8), kind=kLoop, calls=%fused_computation.255 | loop fusion | bytes 64 | tf_op jit(solution)/shard_map/slice | solution.py:78
  1.6 1.6 %fusion.152 = (f32[1]{0:T(128)}, f32[1]{0:T(128)}, f32[1]{0:T(128)}, f32[1]{0:T(128)}, f32[1]{0:T(128)}, /*index=5*/f32[1]{0:T(128)}, f32[1]{0:T(128)}, f32[1]{0:T(128)}) fusion(f32[8]{0:T(128)} %param.7), kind=kLoop, calls=%fused_computation.254 | loop fusion | bytes 64 | tf_op jit(solution)/shard_map/slice | solution.py:78
  3.2 1.6 %fusion.151 = (f32[1]{0:T(128)}, f32[1]{0:T(128)}, f32[1]{0:T(128)}, f32[1]{0:T(128)}, f32[1]{0:T(128)}, /*index=5*/f32[1]{0:T(128)}, f32[1]{0:T(128)}, f32[1]{0:T(128)}) fusion(f32[8]{0:T(128)} %param.9), kind=kLoop, calls=%fused_computation.253 | loop fusion | bytes 64 | tf_op jit(solution)/shard_map/slice | solution.py:78
  4.9 5.7 %select_bitcast_fusion.1 = (f32[1,16,256]{2,1,0:T(8,128)S(1)}, pred[16,256]{1,0:T(8,128)(4,1)S(1)}, pred[16,256]{1,0:T(8,128)(4,1)S(1)}, pred[16,256]{1,0:T(8,12...) fusion(f32[]{:T(128)} %bitcast.7, f32[]{:T(128)} %bitcast.6, ...), kind=kLoop, calls=%fused_computation.117 | loop fusion | flops 65536 | bytes 65568 | tf_op jit(solution)/shard_map/stack | solution.py:91
  10.6 4.9 %select_select_fusion = f32[16,256]{1,0:T(8,128)S(1)} fusion(pred[16,256]{1,0:T(8,128)(4,1)S(1)} %get-tuple-element.19, pred[16,256]{1,0:T(8,128)(4,1)S(1)} %get-tuple-element.18, pred[16,256]{1,0:T(8,128)(4,1)S(1)} %get-tuple-element.17, pred[16,256]{1,0:T(8,128)(4,1)S(1)} %get-tuple-element.16, pred[16,256]{1,0:T(8,128)(4,1)S(1)} %get-tuple-element.15, ...), kind=kLoop, calls=%fused_computation.115 | loop fusion | flops 32768 | bytes 49184 | tf_op jit(solution)/shard_map/jit(_where)/select_n | solution.py:78
  15.4 5.0 %select_bitcast_fusion = f32[1,16,256]{2,1,0:T(8,128)S(1)} fusion(pred[16,256]{1,0:T(8,128)(4,1)S(1)} %get-tuple-element.19, pred[16,256]{1,0:T(8,128)(4,1)S(1)} %get-tuple-element.18, pred[16,256]{1,0:T(8,128)(4,1)S(1)} %get-tuple-element.17, pred[16,256]{1,0:T(8,128)(4,1)S(1)} %get-tuple-element.16, pred[16,256]{1,0:T(8,128)(4,1)S(1)} %get-tuple-element.15, ...), kind=kLoop, calls=%fused_computation.116 | loop fusion | flops 32768 | bytes 49184 | tf_op jit(solution)/shard_map/stack | solution.py:91
  21.0 5.0 %collective-permute-start.1 = (f32[3,2,256]{2,1,0:T(2,128)S(1)}, f32[3,2,256]{2,1,0:T(2,128)S(1)}, u32[]{:S(2)}, u32[]{:S(2)}) collective-permute-start(f32[3,2,256]{2,1,0:T(2,128)S(1)} %get-tuple-element.31), channel_id=1, source_target_pairs={{1,0},{2,1},{3,2},{4,3},{5,4},{6,5},{7,6},{8,7},{9,8},{10,9},{11,1... | collective-permute-start | bytes 18440 | tf_op jit(solution)/shard_map/ppermute | solution.py:23
  26.8 2.8 %reshape_squeeze.4 = f32[2,8,2,128,2]{4,3,2,1,0:T(8,128)S(1)} reshape(f32[1,2,16,256]{3,2,1,0:T(8,128)} %param.5) | data formatting | bytes 65536 | tf_op jit(solution)/shard_map/reshape;squeeze | solution.py:65
  29.7 0.9 %fusion.129 = (f32[2,8,128]{2,1,0:T(8,128)S(1)}, f32[2,8,1,128,1]{4,3,2,1,0:T(8,128)S(1)}) fusion(f32[2,8,2,128,2]{4,3,2,1,0:T(8,128)S(1)} %reshape_squeeze.4), kind=kLoop, calls=%fused_computation.232 | loop fusion | flops 8192 | bytes 49152 | tf_op jit(solution)/shard_map/mul | solution.py:66
  30.6 4.5 %collective-permute-start.3 = (f32[2,1,128]{2,1,0:T(1,128)S(1)}, f32[2,1,128]{2,1,0:T(1,128)S(1)}, u32[]{:S(2)}, u32[]{:S(2)}) collective-permute-start(f32[2,1,128]{2,1,0:T(1,128)S(1)} %get-tuple-element.86), channel_id=1, source_target_pairs={{1,0},{2,1},{3,2},{4,3},{5,4},{6,5},{7,6},{8,7},{9,8},{10,9},{11,1... | collective-permute-start | bytes 3080 | tf_op jit(solution)/shard_map/ppermute | solution.py:23
  36.5 1.2 %collective-permute-done.5 = f32[2,1,256]{2,1,0:T(1,128)S(1)} collective-permute-done((f32[2,1,256]{2,1,0:T(1,128)S(1)}, f32[2,1,256]{2,1,0:T(1,128)S(1)}, u32[]{:S(2)}, u32[]{:S(2)}) %collective-permute-start.5) | collective-permute-done | bytes 2080 | tf_op jit(solution)/shard_map/ppermute | solution.py:23
  38.0 5.9 %reshape.213 = f32[3,10,2,128,2]{4,3,2,1,0:T(8,128)} reshape(f32[3,20,256]{2,1,0:T(8,128)S(1)} %pad_maximum_fusion) | data formatting | bytes 122880 | tf_op jit(solution)/shard_map/reshape | solution.py:65
  43.9 7.1 %fusion.131 = (f32[3,10,1,128,1]{4,3,2,1,0:T(8,128)}, f32[3,10,1,128,1]{4,3,2,1,0:T(8,128)}, f32[3,10,1,128,1]{4,3,2,1,0:T(8,128)}, f32[3,10,1,128,1]{4,3,2,1,0:T(8,128)S(1)}) fusion(f32[3,10,2,128,2]{4,3,2,1,0:T(8,128)} %reshape.213), kind=kLoop, calls=%fused_computation.233 | loop fusion | bytes 122880 | tf_op jit(solution)/shard_map/slice | solution.py:67
  51.1 2.5 %copy.263 = f32[3,10,1,128,1]{3,1,0,4,2:T(8,128)S(1)} copy(f32[3,10,1,128,1]{4,3,2,1,0:T(8,128)} %get-tuple-element.24) | data formatting | bytes 30720
  53.5 2.5 %copy.264 = f32[3,10,1,128,1]{3,1,0,4,2:T(8,128)S(1)} copy(f32[3,10,1,128,1]{4,3,2,1,0:T(8,128)} %get-tuple-element.22) | data formatting | bytes 30720
  56.0 2.5 %copy.265 = f32[3,10,1,128,1]{3,1,0,4,2:T(8,128)S(1)} copy(f32[3,10,1,128,1]{4,3,2,1,0:T(8,128)} %get-tuple-element.23) | data formatting | bytes 30720
  58.4 0.9 %copy.266 = f32[3,10,1,128,1]{3,1,0,4,2:T(8,128)S(1)} copy(f32[3,10,1,128,1]{4,3,2,1,0:T(8,128)S(1)} %get-tuple-element.25) | data formatting | bytes 30720
  60.0 4.4 %collective-permute-start.7 = (f32[2,1,256]{2,1,0:T(1,128)S(1)}, f32[2,1,256]{2,1,0:T(1,128)S(1)}, u32[]{:S(2)}, u32[]{:S(2)}) collective-permute-start(f32[2,1,256]{2,1,0:T(1,128)S(1)} %get-tuple-element.40), channel_id=1, source_target_pairs={{1,0},{2,1},{3,2},{4,3},{5,4},{6,5},{7,6},{8,7},{9,8},{10,9},{11,1... | collective-permute-start | bytes 6152 | tf_op jit(solution)/shard_map/ppermute | solution.py:23
  66.4 3.8 %collective-permute-start.8 = (f32[2,16,256]{2,1,0:T(8,128)S(1)}, f32[2,16,256]{2,1,0:T(8,128)S(1)}, u32[]{:S(2)}, u32[]{:S(2)}) collective-permute-start(f32[2,16,256]{2,1,0:T(8,128)S(1)} %subtract_add_fusion), channel_id=1, source_target_pairs={{0,16},{1,17},{2,18},{3,19},{4,20},{5,21},{6,22},{7,23},{8,24},{9,... | collective-permute-start | bytes 98312 | tf_op jit(solution)/shard_map/ppermute | solution.py:33
  70.4 1.5 %collective-permute-done.8 = f32[2,16,256]{2,1,0:T(8,128)S(1)} collective-permute-done((f32[2,16,256]{2,1,0:T(8,128)S(1)}, f32[2,16,256]{2,1,0:T(8,128)S(1)}, u32[]{:S(2)}, u32[]{:S(2)}) %collective-permute-start.8) | collective-permute-done | bytes 32800 | tf_op jit(solution)/shard_map/ppermute | solution.py:33
  71.9 2.1 %reshape.216 = f32[2,8,2,128,2]{4,3,2,1,0:T(8,128)S(1)} reshape(f32[2,16,256]{2,1,0:T(8,128)S(1)} %broadcast_select_fusion) | data formatting | bytes 65536 | tf_op jit(solution)/shard_map/reshape | solution.py:65
  73.9 0.9 %fusion.127 = (f32[2,8,128]{2,1,0:T(8,128)S(1)}, f32[2,8,1,128,1]{4,3,2,1,0:T(8,128)S(1)}) fusion(f32[2,8,2,128,2]{4,3,2,1,0:T(8,128)S(1)} %reshape.216), kind=kLoop, calls=%fused_computation.231 | loop fusion | flops 8192 | bytes 49152 | tf_op jit(solution)/shard_map/mul | solution.py:66
  74.9 3.6 %collective-permute-start.10 = (f32[2,1,128]{2,1,0:T(1,128)S(1)}, f32[2,1,128]{2,1,0:T(1,128)S(1)}, u32[]{:S(2)}, u32[]{:S(2)}) collective-permute-start(f32[2,1,128]{2,1,0:T(1,128)S(1)} %get-tuple-element.74), channel_id=1, source_target_pairs={{1,0},{2,1},{3,2},{4,3},{5,4},{6,5},{7,6},{8,7},{9,8},{10,9},{11,1... | collective-permute-start | bytes 3080 | tf_op jit(solution)/shard_map/ppermute | solution.py:23
  79.8 4.4 %collective-permute-done.9 = f32[2,1,128]{2,1,0:T(1,128)S(1)} collective-permute-done((f32[2,1,128]{2,1,0:T(1,128)S(1)}, f32[2,1,128]{2,1,0:T(1,128)S(1)}, u32[]{:S(2)}, u32[]{:S(2)}) %collective-permute-start.9) | collective-permute-done | bytes 1056 | tf_op jit(solution)/shard_map/ppermute | solution.py:21
  (93 shorter events, 8.4 us)
Async XLA Ops:
  20.5 17.2 %collective-permute-start = (f32[3,2,256]{2,1,0:T(2,128)S(1)}, f32[3,2,256]{2,1,0:T(2,128)S(1)}, u32[]{:S(2)}, u32[]{:S(2)}) collective-permute-start(f32[3,2,256]{2,1,0:T(2,128)S(1)} %get-tuple-element.30), channel_id=1, source_target_pairs={{0,1},{1,2},{2,3},{3,4},{4,5},{5,6},{6,7},{7,8},{8,9},{9,10},{10,1... | collective-permute-start | bytes 18440 | tf_op jit(solution)/shard_map/ppermute | solution.py:21
  21.0 16.7 %collective-permute-start.1 = (f32[3,2,256]{2,1,0:T(2,128)S(1)}, f32[3,2,256]{2,1,0:T(2,128)S(1)}, u32[]{:S(2)}, u32[]{:S(2)}) collective-permute-start(f32[3,2,256]{2,1,0:T(2,128)S(1)} %get-tuple-element.31), channel_id=1, source_target_pairs={{1,0},{2,1},{3,2},{4,3},{5,4},{6,5},{7,6},{8,7},{9,8},{10,9},{11,1... | collective-permute-start | bytes 18440 | tf_op jit(solution)/shard_map/ppermute | solution.py:23
  26.8 9.7 %collective-permute-start.4 = (f32[2,1,256]{2,1,0:T(1,128)S(1)}, f32[2,1,256]{2,1,0:T(1,128)S(1)}, u32[]{:S(2)}, u32[]{:S(2)}) collective-permute-start(f32[2,1,256]{2,1,0:T(1,128)S(1)} %get-tuple-element.45), channel_id=1, source_target_pairs={{0,1},{1,2},{2,3},{3,4},{4,5},{5,6},{6,7},{7,8},{8,9},{9,10},{10,1... | collective-permute-start | bytes 6152 | tf_op jit(solution)/shard_map/ppermute | solution.py:21
  29.6 5.5 %copy-start = (f32[1,2,16,256]{3,2,1,0:T(8,128)S(1)}, f32[1,2,16,256]{3,2,1,0:T(8,128)}, u32[]{:S(2)}) copy-start(f32[1,2,16,256]{3,2,1,0:T(8,128)} %param.5) | copy-start | bytes 98308
  30.6 5.8 %collective-permute-start.2 = (f32[2,1,128]{2,1,0:T(1,128)S(1)}, f32[2,1,128]{2,1,0:T(1,128)S(1)}, u32[]{:S(2)}, u32[]{:S(2)}) collective-permute-start(f32[2,1,128]{2,1,0:T(1,128)S(1)} %get-tuple-element.87), channel_id=1, source_target_pairs={{0,1},{1,2},{2,3},{3,4},{4,5},{5,6},{6,7},{7,8},{8,9},{9,10},{10,1... | collective-permute-start | bytes 3080 | tf_op jit(solution)/shard_map/ppermute | solution.py:21
  30.6 5.8 %collective-permute-start.3 = (f32[2,1,128]{2,1,0:T(1,128)S(1)}, f32[2,1,128]{2,1,0:T(1,128)S(1)}, u32[]{:S(2)}, u32[]{:S(2)}) collective-permute-start(f32[2,1,128]{2,1,0:T(1,128)S(1)} %get-tuple-element.86), channel_id=1, source_target_pairs={{1,0},{2,1},{3,2},{4,3},{5,4},{6,5},{7,6},{8,7},{9,8},{10,9},{11,1... | collective-permute-start | bytes 3080 | tf_op jit(solution)/shard_map/ppermute | solution.py:23
  36.3 1.3 %collective-permute-start.5 = (f32[2,1,256]{2,1,0:T(1,128)S(1)}, f32[2,1,256]{2,1,0:T(1,128)S(1)}, u32[]{:S(2)}, u32[]{:S(2)}) collective-permute-start(f32[2,1,256]{2,1,0:T(1,128)S(1)} %get-tuple-element.44), channel_id=1, source_target_pairs={{1,0},{2,1},{3,2},{4,3},{5,4},{6,5},{7,6},{8,7},{9,8},{10,9},{11,1... | collective-permute-start | bytes 6152 | tf_op jit(solution)/shard_map/ppermute | solution.py:23
  60.0 5.8 %collective-permute-start.6 = (f32[2,1,256]{2,1,0:T(1,128)S(1)}, f32[2,1,256]{2,1,0:T(1,128)S(1)}, u32[]{:S(2)}, u32[]{:S(2)}) collective-permute-start(f32[2,1,256]{2,1,0:T(1,128)S(1)} %get-tuple-element.41), channel_id=1, source_target_pairs={{0,1},{1,2},{2,3},{3,4},{4,5},{5,6},{6,7},{7,8},{8,9},{9,10},{10,1... | collective-permute-start | bytes 6152 | tf_op jit(solution)/shard_map/ppermute | solution.py:21
  60.0 5.8 %collective-permute-start.7 = (f32[2,1,256]{2,1,0:T(1,128)S(1)}, f32[2,1,256]{2,1,0:T(1,128)S(1)}, u32[]{:S(2)}, u32[]{:S(2)}) collective-permute-start(f32[2,1,256]{2,1,0:T(1,128)S(1)} %get-tuple-element.40), channel_id=1, source_target_pairs={{1,0},{2,1},{3,2},{4,3},{5,4},{6,5},{7,6},{8,7},{9,8},{10,9},{11,1... | collective-permute-start | bytes 6152 | tf_op jit(solution)/shard_map/ppermute | solution.py:23
  66.4 5.4 %collective-permute-start.8 = (f32[2,16,256]{2,1,0:T(8,128)S(1)}, f32[2,16,256]{2,1,0:T(8,128)S(1)}, u32[]{:S(2)}, u32[]{:S(2)}) collective-permute-start(f32[2,16,256]{2,1,0:T(8,128)S(1)} %subtract_add_fusion), channel_id=1, source_target_pairs={{0,16},{1,17},{2,18},{3,19},{4,20},{5,21},{6,22},{7,23},{8,24},{9,... | collective-permute-start | bytes 98312 | tf_op jit(solution)/shard_map/ppermute | solution.py:33
  74.9 4.9 %collective-permute-start.10 = (f32[2,1,128]{2,1,0:T(1,128)S(1)}, f32[2,1,128]{2,1,0:T(1,128)S(1)}, u32[]{:S(2)}, u32[]{:S(2)}) collective-permute-start(f32[2,1,128]{2,1,0:T(1,128)S(1)} %get-tuple-element.74), channel_id=1, source_target_pairs={{1,0},{2,1},{3,2},{4,3},{5,4},{6,5},{7,6},{8,7},{9,8},{10,9},{11,1... | collective-permute-start | bytes 3080 | tf_op jit(solution)/shard_map/ppermute | solution.py:23
  78.5 5.7 %collective-permute-start.9 = (f32[2,1,128]{2,1,0:T(1,128)S(1)}, f32[2,1,128]{2,1,0:T(1,128)S(1)}, u32[]{:S(2)}, u32[]{:S(2)}) collective-permute-start(f32[2,1,128]{2,1,0:T(1,128)S(1)} %get-tuple-element.75), channel_id=1, source_target_pairs={{0,1},{1,2},{2,3},{3,4},{4,5},{5,6},{6,7},{7,8},{8,9},{9,10},{10,1... | collective-permute-start | bytes 3080 | tf_op jit(solution)/shard_map/ppermute | solution.py:21
where the time goes:
time: 86.3 us; the launch traced here: 85.7 us
  local copies, waits for them, and re-layouts  35.3 us (41%)
  starting transfers between devices  22.1 us (26%)
  other arithmetic  18.9 us (22%)
  waiting for transfers between devices  9.13 us (11%)
    ppermute x5, starting transfers between devices, with_halo(): lax.ppermute(head, axis, [((i + 1) % count, i) for i in range(count)])  17.6 us
    another operation x2, other arithmetic, on_device(): jnp.stack([lookup(prey_motility, habitat), lookup(predator_motility, habi...  10.7 us
    unnamed x6, local copies, waits for them, and re-layouts  8.31 us
    reshape x2, local copies, waits for them, and re-layouts, restrict(): blocks = field.reshape(shape[:-2] + (shape[-2] // 2, 2, shape[-1] // 2, 2))  7.98 us
    slice x1, local copies, waits for them, and re-layouts, restrict(): blocks[..., 0, :, 1]  7.13 us
    ppermute x5, waiting for transfers between devices, with_halo(): lax.ppermute(tail, axis, [(i, (i + 1) % count) for i in range(count)])  5.49 us
    select_n x1, other arithmetic, lookup(): result = jnp.where(habitat == klass, table[klass], result)  4.86 us
    slice x3, local copies, waits for them, and re-layouts, lookup(): result = jnp.where(habitat == klass, table[klass], result)  4.86 us
  transfers between devices with their start and end apart: 11, of which 8 were waited for; matrix products, arithmetic and copies ran while one was open for 7% of the time, Pallas kernels for 0%

commit v1 on v0

v1 whole, which is shorter than its diff:
```python
import functools

import jax
import jax.numpy as jnp
from jax import lax
from jax.experimental import pallas as pl
from jax.experimental.pallas import tpu as pltpu
from jax.sharding import PartitionSpec as P

GROWTH = 0.5
ATTACK = 0.5
HANDLING = 1.0
CONVERSION = 0.6
MORTALITY = 0.3
TAXIS = 0.15

EDGE = 4
TILE = 8


def at(field, by, axis):
    return pltpu.roll(field, (-by) % field.shape[axis], axis)


def laplace(field, by):
    return (
        at(field, by, 0) + at(field, -by, 0) + at(field, by, 1) + at(field, -by, 1) - 4.0 * field
    )


def advance(state, coefs, step_dt, inv_h2, by):
    prey, predator = state
    prey_mob, pred_mob, capacity = coefs
    spread_prey = laplace(prey_mob * prey, by) * inv_h2
    spread_pred = laplace(pred_mob * predator, by) * inv_h2
    row_flux = 0.5 * (predator + at(predator, by, 0)) * (at(prey, by, 0) - prey)
    col_flux = 0.5 * (predator + at(predator, by, 1)) * (at(prey, by, 1) - prey)
    taxis_div = (row_flux - at(row_flux, -by, 0) + col_flux - at(col_flux, -by, 1)) * inv_h2
    response = prey * predator / (1.0 + HANDLING * jnp.abs(prey))
    new_prey = prey + step_dt * (
        spread_prey + GROWTH * prey * (1.0 - prey / capacity) - ATTACK * response
    )
    new_pred = predator + step_dt * (
        spread_pred - TAXIS * taxis_div + CONVERSION * ATTACK * response - MORTALITY * predator
    )
    return new_prey, new_pred


def block_mean(field):
    for axis in (0, 1):
        even = lax.broadcasted_iota(jnp.int32, field.shape, axis) % 2 == 0
        field = field + jnp.where(even, at(field, 1, axis), at(field, -1, axis))
    return field * 0.25


def fine_pair(state, coefs):
    for _ in range(2):
        state = advance(state, coefs, 1.0, 1.0, 1)
    return state


def coarse_prop(state, coarse_coefs):
    return advance(tuple(map(block_mean, state)), coarse_coefs, 2.0, 0.25, 2)


def edge_tile(strip):
    head = lax.broadcasted_iota(jnp.int32, (TILE, strip.shape[1]), 0) < EDGE
    return jnp.where(head, strip[:TILE], strip[strip.shape[0] - TILE :])


def widened(strip, after, before, swapped):
    head = lax.broadcasted_iota(jnp.int32, after.shape, 0) < EDGE
    if swapped:
        head = head == (lax.axis_index("space") % 2 == 0)
    return jnp.concatenate([strip, jnp.where(head, after, before)], axis=0)


def lookup(table_ref, habitat):
    result = jnp.full(habitat.shape, table_ref[0], jnp.float32)
    for klass in range(1, table_ref.shape[0]):
        result = jnp.where(habitat == klass, table_ref[klass], result)
    return result


def edges_kernel(*refs):
    *strips, out_ref = refs
    place = 0
    for ref in strips:
        for k in range(ref.shape[1] if len(ref.shape) == 4 else 1):
            strip = ref[0, k] if len(ref.shape) == 4 else ref[...]
            out_ref[place] = edge_tile(strip).astype(jnp.float32)
            place += 1


def strip_kernel(
    own_ref,
    prev_ref,
    habitat_ref,
    after_ref,
    before_ref,
    prey_ref,
    pred_ref,
    cap_ref,
    end_ref,
    *correction_refs,
    swapped,
):
    def wide(strip, k):
        return widened(strip, after_ref[k], before_ref[k], swapped)

    own = tuple(wide(own_ref[0, k], k) for k in range(2))
    prev = tuple(wide(prev_ref[0, k], 2 + k) for k in range(2))
    habitat = wide(habitat_ref[...].astype(jnp.float32), 4)
    coefs = tuple(lookup(ref, habitat) for ref in (prey_ref, pred_ref, cap_ref))
    coarse_coefs = tuple(map(block_mean, coefs))

    def corrections(start):
        coarse = coarse_prop(start, coarse_coefs)
        return coarse, tuple(f - g for f, g in zip(fine_pair(start, coefs), coarse))

    own_coarse, correction = corrections(own)
    prev_coarse, prev_correction = corrections(prev)
    first_end = tuple(g + c for g, c in zip(prev_coarse, prev_correction))
    handed = coarse_prop(first_end, coarse_coefs)
    first = lax.axis_index("tm") == 0
    rows = habitat_ref.shape[0]
    for k in range(2):
        end = jnp.where(first, own_coarse[k], handed[k]) + correction[k]
        end_ref[0, k] = end[:rows]
        for ref in correction_refs:
            ref[0, k] = correction[k][:rows]


def hand_kernel(
    end_ref,
    correction_ref,
    arrived_ref,
    habitat_ref,
    after_ref,
    before_ref,
    prey_ref,
    pred_ref,
    cap_ref,
    out_ref,
    *,
    swapped,
    taker,
):
    rows = habitat_ref.shape[0]
    arrived = tuple(
        widened(arrived_ref[0, k], after_ref[k], before_ref[k], swapped) for k in range(2)
    )
    habitat = widened(habitat_ref[...].astype(jnp.float32), after_ref[2], before_ref[2], swapped)
    coefs = tuple(lookup(ref, habitat) for ref in (prey_ref, pred_ref, cap_ref))
    handed = coarse_prop(arrived, tuple(map(block_mean, coefs)))
    takes = lax.axis_index("tm") == taker
    for k in range(2):
        out_ref[0, k] = jnp.where(takes, handed[k][:rows] + correction_ref[0, k], end_ref[0, k])


def local_call(kernel, outs, arrays, tables=()):
    vmem, smem = pl.BlockSpec(memory_space=pltpu.VMEM), pl.BlockSpec(memory_space=pltpu.SMEM)
    return pl.pallas_call(
        kernel,
        out_shape=[jax.ShapeDtypeStruct(shape, jnp.float32) for shape in outs],
        in_specs=[vmem] * len(arrays) + [smem] * len(tables),
        out_specs=[vmem] * len(outs),
        compiler_params=pltpu.CompilerParams(vmem_limit_bytes=4 * 2**20),
    )(*arrays, *tables)


def both_neighbours(tile):
    count = lax.axis_size("space")
    ring = [(i, (i + 1) % count) for i in range(count)]
    if count % 2:
        return (
            lax.ppermute(tile, "space", [(j, i) for i, j in ring]),
            lax.ppermute(tile, "space", ring),
            False,
        )
    swaps = [[pair for i, j in ring[start::2] for pair in ((i, j), (j, i))] for start in (0, 1)]
    outer = lax.ppermute(tile, "space", swaps[1])
    inner = lax.ppermute(tile, "space", swaps[0])
    return inner, outer, True


def from_behind(array):
    count = lax.axis_size("tm")
    return lax.ppermute(array, "tm", [(i, i + 1) for i in range(count - 1)])


def on_device(slice_starts, habitat, capacity_table, prey_motility, predator_motility):
    shape = slice_starts.shape
    tables = prey_motility, predator_motility, capacity_table
    slices = lax.axis_size("tm")
    previous = from_behind(slice_starts)
    (edges,) = local_call(
        edges_kernel, [(5, TILE, shape[-1])], [slice_starts, previous, habitat]
    )
    after, before, swapped = both_neighbours(edges)
    end, *correction = local_call(
        functools.partial(strip_kernel, swapped=swapped),
        [shape] * (1 if slices <= 2 else 2),
        [slice_starts, previous, habitat, after, before],
        tables,
    )
    for taker in range(2, slices):
        arrived = from_behind(end)
        (edges,) = local_call(edges_kernel, [(3, TILE, shape[-1])], [arrived, habitat])
        after, before, swapped = both_neighbours(edges)
        (end,) = local_call(
            functools.partial(hand_kernel, swapped=swapped, taker=taker),
            [shape],
            [end, *correction, arrived, habitat, after, before],
            tables,
        )
    return end


def solution(mesh):
    placed = (P("tm", None, "space", None), P("space", None), P(), P(), P())
    return jax.shard_map(
        on_device,
        mesh=mesh,
        in_specs=placed,
        out_specs=P("tm", None, "space", None),
        check_vma=False,
    )
```

time: 86.3 us -> 16.8 us (0.19)
  local copies, waits for them, and re-layouts: 35.3 us -> 1.49 us
  other arithmetic: 18.9 us -> 0 us
  starting transfers between devices: 22.1 us -> 8.07 us
  waiting for transfers between devices: 9.13 us -> 4.9 us
  Pallas kernels: 0 us -> 2.04 us
    slice x42 -> x0, local copies, waits for them, and re-layouts: 15.4 us -> none  [the longest x1 7.13 us: restrict(): blocks[..., 0, :, 1]]
    ppermute x11 -> x3, starting transfers between devices: 22.1 us -> 8.07 us  [the longest x1 4.89 us: from_behind(): return lax.ppermute(array, 'tm', [(i, i + 1) for i in range(count - 1)])]
    another operation x8 -> x0, other arithmetic: 11.1 us -> none  [the longest x2 10.7 us: on_device(): jnp.stack([lookup(prey_motility, habitat), lookup(predator_motility, habi...]
    reshape x7 -> x0, local copies, waits for them, and re-layouts: 8.46 us -> none  [the longest x2 7.98 us: restrict(): blocks = field.reshape(shape[:-2] + (shape[-2] // 2, 2, shape[-1] // 2, 2))]
    unnamed x6 -> x10, local copies, waits for them, and re-layouts: 8.31 us -> 1.49 us
    select_n x3 -> x0, other arithmetic: 4.88 us -> none  [the longest x1 4.86 us: lookup(): result = jnp.where(habitat == klass, table[klass], result)]
    ppermute x11 -> x3, waiting for transfers between devices: 9.13 us -> 4.9 us  [the longest x1 3.01 us: both_neighbours(): outer = lax.ppermute(tile, 'space', swaps[1])]
    another operation x1 -> x0, local copies, waits for them, and re-layouts: 2.84 us -> none  [restrict(): blocks = field.reshape(shape[:-2] + (shape[-2] // 2, 2, shape[-1] // 2, 2))]
  transfers between devices with their start and end apart: 11 -> 3, of which waited for: 8 -> 2; matrix products, arithmetic and copies ran while one was open for 7% -> 0% of each run, Pallas kernels for 0% -> 0%
where the time goes in v1:
time: 16.8 us; the launch traced here: 16.5 us
  starting transfers between devices  8.07 us (48%)
  waiting for transfers between devices  4.9 us (29%)
  Pallas kernels  2.04 us (12%)
  local copies, waits for them, and re-layouts  1.49 us (9%)
    ppermute x1, starting transfers between devices, from_behind(): return lax.ppermute(array, 'tm', [(i, i + 1) for i in range(count - 1)])  4.89 us
    ppermute x1, starting transfers between devices, both_neighbours(): outer = lax.ppermute(tile, 'space', swaps[1])  3.18 us
    ppermute x1, waiting for transfers between devices, both_neighbours(): outer = lax.ppermute(tile, 'space', swaps[1])  3.01 us
    pallas_call x2, Pallas kernels, local_call(): pl.pallas_call(kernel, out_shape=[jax.ShapeDtypeStruct(shape, jnp.float32...  2.04 us
    ppermute x1, waiting for transfers between devices, from_behind(): return lax.ppermute(array, 'tm', [(i, i + 1) for i in range(count - 1)])  1.89 us
    unnamed x10, local copies, waits for them, and re-layouts  1.49 us
  transfers between devices with their start and end apart: 3, of which 2 were waited for; matrix products, arithmetic and copies ran while one was open for 0% of the time, Pallas kernels for 0%

profile of v1, /device:TPU:0, one launch (start us, length us, event | category | flops | bytes accessed | tf_op | source)
XLA Modules:
  0.0 16.5 jit_solution(2509357601079724689)
XLA Ops:
  0.0 4.9 %collective-permute-start = (f32[1,2,16,256]{3,2,1,0:T(8,128)}, f32[1,2,16,256]{3,2,1,0:T(8,128)S(1)}, u32[]{:S(2)}, u32[]{:S(2)}) collective-permute-start(f32[1,2,16,256]{3,2,1,0:T(8,128)} %own_ref.1), channel_id=1, source_target_pairs={{0,16},{1,17},{2,18},{3,19},{4,20},{5,21},{6,22},{7,23},{8,24},{9,... | collective-permute-start | bytes 98312 | tf_op jit(solution)/shard_map/ppermute | solution.py:189
  4.9 1.9 %collective-permute-done.refs_1_.prev_ref = f32[1,2,16,256]{3,2,1,0:T(8,128)S(1)} collective-permute-done((f32[1,2,16,256]{3,2,1,0:T(8,128)}, f32[1,2,16,256]{3,2,1,0:T(8,128)S(1)}, u32[]{:S(2)}, u32[]{:S(2)}) %collective-permute-start) | collective-permute-done | bytes 32800 | tf_op jit(solution)/shard_map/ppermute | solution.py:189
  6.8 0.0 copy-start
  6.8 0.8 %copy-done = f32[1,2,16,256]{3,2,1,0:T(8,128)S(1)} copy-done((f32[1,2,16,256]{3,2,1,0:T(8,128)S(1)}, f32[1,2,16,256]{3,2,1,0:T(8,128)}, u32[]{:S(2)}) %copy-start) | copy-done | bytes 32792
  7.5 0.0 copy-start.1
  7.6 0.7 %copy-done.1 = s32[16,256]{1,0:T(8,128)S(1)} copy-done((s32[16,256]{1,0:T(8,128)S(1)}, s32[16,256]{1,0:T(8,128)}, u32[]{:S(2)}) %copy-start.1) | copy-done | bytes 16408
  8.3 0.0 copy-start.2
  8.3 0.0 copy-start.3
  8.3 0.0 copy-start.4
  8.3 3.2 %collective-permute-start.2 = (f32[5,8,256]{2,1,0:T(8,128)S(1)}, f32[5,8,256]{2,1,0:T(8,128)S(1)}, u32[]{:S(2)}, u32[]{:S(2)}) collective-permute-start(f32[5,8,256]{2,1,0:T(8,128)S(1)} %shard_map.55), channel_id=1, source_target_pairs={{1,2},{2,1},{3,4},{4,3},{5,6},{6,5},{7,8},{8,7},{9,10},{10,9},{11,... | collective-permute-start | bytes 122888 | tf_op jit(solution)/shard_map/ppermute | solution.py:182
  11.5 0.0 collective-permute-start.1
  11.5 3.0 %collective-permute-done.2.before_ref = f32[5,8,256]{2,1,0:T(8,128)S(1)} collective-permute-done((f32[5,8,256]{2,1,0:T(8,128)S(1)}, f32[5,8,256]{2,1,0:T(8,128)S(1)}, u32[]{:S(2)}, u32[]{:S(2)}) %collective-permute-start.2) | collective-permute-done | bytes 40992 | tf_op jit(solution)/shard_map/ppermute | solution.py:182
  14.5 0.0 collective-permute-done.1.after_ref
  14.5 0.0 copy-done.2
  14.5 0.0 copy-done.3
  14.5 0.0 copy-done.4
  14.5 2.0 %shard_map.56 = f32[1,2,16,256]{3,2,1,0:T(8,128)} custom-call(f32[1,2,16,256]{3,2,1,0:T(8,128)S(1)} %copy-done, f32[1,2,16,256]{3,2,1,0:T(8,128)S(1)} %collective-permute-done.refs_1_.prev_ref, s32[16,256]{1,0:T(8,128)S(1)} %copy-done.1, f32[5,8,256]{2,1,0:T(8,128)S(1)} %collective-permute-done.1.after_ref, ...), custom_call_target="tpu_custom_call" | custom-call | tf_op jit(solution)/shard_map/pallas_call | solution.py:163
  (1 shorter events, 0.0 us)
Async XLA Ops:
  0.0 6.8 %collective-permute-start = (f32[1,2,16,256]{3,2,1,0:T(8,128)}, f32[1,2,16,256]{3,2,1,0:T(8,128)S(1)}, u32[]{:S(2)}, u32[]{:S(2)}) collective-permute-start(f32[1,2,16,256]{3,2,1,0:T(8,128)} %own_ref.1), channel_id=1, source_target_pairs={{0,16},{1,17},{2,18},{3,19},{4,20},{5,21},{6,22},{7,23},{8,24},{9,... | collective-permute-start | bytes 98312 | tf_op jit(solution)/shard_map/ppermute | solution.py:189
  6.8 0.8 %copy-start = (f32[1,2,16,256]{3,2,1,0:T(8,128)S(1)}, f32[1,2,16,256]{3,2,1,0:T(8,128)}, u32[]{:S(2)}) copy-start(f32[1,2,16,256]{3,2,1,0:T(8,128)} %own_ref.1) | copy-start | bytes 98308
  7.5 0.7 %copy-start.1 = (s32[16,256]{1,0:T(8,128)S(1)}, s32[16,256]{1,0:T(8,128)}, u32[]{:S(2)}) copy-start(s32[16,256]{1,0:T(8,128)} %habitat_ref.1) | copy-start | bytes 49156
  8.3 6.2 %copy-start.2 = (f32[8]{0:T(128)S(1)}, f32[8]{0:T(128)}, u32[]{:S(2)}) copy-start(f32[8]{0:T(128)} %prey_ref.1) | copy-start | bytes 100
  8.3 6.2 %copy-start.3 = (f32[8]{0:T(128)S(1)}, f32[8]{0:T(128)}, u32[]{:S(2)}) copy-start(f32[8]{0:T(128)} %pred_ref.1) | copy-start | bytes 100
  8.3 6.2 %copy-start.4 = (f32[8]{0:T(128)S(1)}, f32[8]{0:T(128)}, u32[]{:S(2)}) copy-start(f32[8]{0:T(128)} %cap_ref.1) | copy-start | bytes 100
  8.3 6.2 %collective-permute-start.2 = (f32[5,8,256]{2,1,0:T(8,128)S(1)}, f32[5,8,256]{2,1,0:T(8,128)S(1)}, u32[]{:S(2)}, u32[]{:S(2)}) collective-permute-start(f32[5,8,256]{2,1,0:T(8,128)S(1)} %shard_map.55), channel_id=1, source_target_pairs={{1,2},{2,1},{3,4},{4,3},{5,6},{6,5},{7,8},{8,7},{9,10},{10,9},{11,... | collective-permute-start | bytes 122888 | tf_op jit(solution)/shard_map/ppermute | solution.py:182
  11.5 3.0 %collective-permute-start.1 = (f32[5,8,256]{2,1,0:T(8,128)S(1)}, f32[5,8,256]{2,1,0:T(8,128)S(1)}, u32[]{:S(2)}, u32[]{:S(2)}) collective-permute-start(f32[5,8,256]{2,1,0:T(8,128)S(1)} %shard_map.55), channel_id=1, source_target_pairs={{0,1},{1,0},{2,3},{3,2},{4,5},{5,4},{6,7},{7,6},{8,9},{9,8},{10,11... | collective-permute-start | bytes 122888 | tf_op jit(solution)/shard_map/ppermute | solution.py:183

commit v2 on v1

v2 whole, which is shorter than its diff:
```python
import functools

import jax
import jax.numpy as jnp
from jax import lax
from jax.experimental import pallas as pl
from jax.experimental.pallas import tpu as pltpu
from jax.sharding import PartitionSpec as P

GROWTH = 0.5
ATTACK = 0.5
HANDLING = 1.0
CONVERSION = 0.6
MORTALITY = 0.3
TAXIS = 0.15

EDGE = 4
TILE = 8
FINE = (1.0, 1.0)
COARSE = (2.0, 0.25)


def lanes(shape):
    return lax.broadcasted_iota(jnp.int32, shape, len(shape) - 1)


def take(field, index):
    return jnp.take_along_axis(field, index, axis=1, mode="promise_in_bounds")


def split(field):
    half = field.shape[1] // 2
    low, high = field[:, :half], field[:, half:]
    lane = lanes(low.shape)
    source = (2 * lane) % half
    return tuple(
        jnp.where(lane < half // 2, take(low, source + odd), take(high, source + odd))
        for odd in (0, 1)
    )


def joined(even, odd):
    half = even.shape[1]
    lane = lanes(even.shape)
    parts = []
    for first in (0, half // 2):
        source = lane // 2 + first
        part = take(even, source)
        if odd is not even:
            part = jnp.where(lane % 2 == 0, part, take(odd, source))
        parts.append(part)
    return jnp.concatenate(parts, axis=1)


def each(function, *fields):
    return tuple(map(function, *fields))


def shift(array, by, axis):
    return pltpu.roll(array, (-by) % array.shape[axis], axis)


def following(field):
    return (*field[1:], shift(field[0], 1, 1))


def preceding(field):
    return (shift(field[-1], -1, 1), *field[:-1])


def laplace(field, by):
    return each(
        lambda c, n, p: (shift(c, by, 0) + shift(c, -by, 0)) + (n + p) - 4.0 * c,
        field,
        following(field),
        preceding(field),
    )


def advance(prey, predator, prey_mob, pred_mob, inv_capacity, scales):
    step_dt, inv_h2 = scales
    by = 3 - len(prey)
    spread_prey = laplace(each(jnp.multiply, prey_mob, prey), by)
    spread_pred = laplace(each(jnp.multiply, pred_mob, predator), by)

    def flux(prey_here, pred_here, prey_next, pred_next):
        return (pred_here + pred_next) * (prey_next - prey_here)

    rows_on = [each(lambda c: shift(c, by, 0), field) for field in (prey, predator)]
    row_flux = each(flux, prey, predator, *rows_on)
    col_flux = each(flux, prey, predator, following(prey), following(predator))
    taxis_div = each(
        lambda r, c, p: (r - shift(r, -by, 0)) + (c - p), row_flux, col_flux, preceding(col_flux)
    )
    response = each(lambda u, v: u * v / (1.0 + HANDLING * jnp.abs(u)), prey, predator)
    new_prey = each(
        lambda u, s, k, r: (
            u + s + (step_dt * GROWTH) * (u * (1.0 - u * k)) - (step_dt * ATTACK) * r
        ),
        prey,
        spread_prey,
        inv_capacity,
        response,
    )
    new_pred = each(
        lambda v, s, d, r: (
            (1.0 - step_dt * MORTALITY) * v
            + s
            - (0.5 * TAXIS * step_dt * inv_h2) * d
            + (step_dt * CONVERSION * ATTACK) * r
        ),
        predator,
        spread_pred,
        taxis_div,
        response,
    )
    return new_prey, new_pred


def restrict(field):
    even, odd = field
    total = even + odd
    row = lax.broadcasted_iota(jnp.int32, total.shape, 0)
    partner = jnp.where(row % 2 == 0, shift(total, 1, 0), shift(total, -1, 0))
    return ((total + partner) * 0.25,)


def edge_tile(strip):
    head = lax.broadcasted_iota(jnp.int32, (TILE, strip.shape[1]), 0) < EDGE
    return jnp.where(head, strip[:TILE], strip[strip.shape[0] - TILE :])


def halo(after, before, swapped):
    head = lax.broadcasted_iota(jnp.int32, after.shape, 0) < EDGE
    if swapped:
        head = head == (lax.axis_index("space") % 2 == 0)
    return jnp.where(head, after, before)


def halves(array):
    half = array.shape[-1] // 2
    return array[:, :half], array[:, half:]


def load_kernel(starts_hbm, habitat_hbm, edges_ref, strip_ref, starts_ref, habitat_ref, sem):
    copies = [
        pltpu.make_async_copy(starts_hbm, starts_ref, sem.at[0]),
        pltpu.make_async_copy(habitat_hbm, habitat_ref, sem.at[1]),
    ]
    for copy in copies:
        copy.start()
    for copy in copies:
        copy.wait()
    fields = [starts_ref[0, 0], starts_ref[0, 1], habitat_ref[...].astype(jnp.float32)]
    for k, field in enumerate(fields):
        edges_ref[k] = jnp.concatenate(split(edge_tile(field)), axis=1)
        strip_ref[k] = field


def lookups(tables, habitat):
    index = habitat.astype(jnp.int32)
    return [take(jnp.broadcast_to(table[:1], index.shape), index) for table in tables]


def prepare_kernel(strip_ref, prey_ref, pred_ref, cap_ref, fields_ref, coefs_ref, tables_ref):
    lane = lanes(tables_ref.shape[1:])
    tables = []
    for ref in (prey_ref, pred_ref, cap_ref):
        table = jnp.full(lane.shape, ref[0], jnp.float32)
        for klass in range(1, ref.shape[0]):
            table = jnp.where(lane == klass, ref[klass], table)
        tables.append(table)
    tables.append(1.0 / tables[2])
    for k, table in enumerate(tables):
        tables_ref[k] = table
    half = fields_ref.shape[2] // 2
    for k in range(2):
        fields_ref[k] = jnp.concatenate(split(strip_ref[k]), axis=1)
    for part, habitat in enumerate(split(strip_ref[2])):
        for k, coef in enumerate(lookups(tables, habitat)):
            coefs_ref[k, :, part * half : (part + 1) * half] = coef


def propagate_kernel(
    fields_ref,
    coefs_ref,
    tables_ref,
    after_ref,
    before_ref,
    coarse_end_ref,
    coarse_coefs_ref,
    coarse_correction_ref,
    correction_ref,
    end_ref,
    *,
    swapped,
):
    def wide(strip, edge):
        return each(lambda *parts: jnp.concatenate(parts, axis=0), halves(strip), halves(edge))

    edges = [halo(after_ref[k], before_ref[k], swapped) for k in range(3)]
    prey, predator = (wide(fields_ref[k], edges[k]) for k in range(2))
    tables = [tables_ref[k] for k in range(4)]
    edge_coefs = zip(*(lookups(tables, part) for part in halves(edges[2])))
    coefs = [
        wide(coefs_ref[k], jnp.concatenate(edge, axis=1)) for k, edge in enumerate(edge_coefs)
    ]
    prey_mob, pred_mob, capacity, inv_capacity = coefs
    scale = COARSE[0] * COARSE[1]
    coarse_coefs = (
        each(lambda c: scale * c, restrict(prey_mob)),
        each(lambda c: scale * c, restrict(pred_mob)),
        each(lambda c: 1.0 / c, restrict(capacity)),
    )
    coarse = advance(restrict(prey), restrict(predator), *coarse_coefs, COARSE)
    fine = prey, predator
    for _ in range(2):
        fine = advance(*fine, prey_mob, pred_mob, inv_capacity, FINE)
    rows = fields_ref.shape[1]
    for k in range(2):
        correction = each(lambda f: f - coarse[k][0], fine[k])
        end = each(lambda c: coarse[k][0] + c, correction)
        coarse_end_ref[k] = restrict(end)[0]
        coarse_correction_ref[k] = restrict(correction)[0][:rows]
        correction_ref[k] = jnp.concatenate(correction, axis=1)[:rows]
        end_ref[k] = jnp.concatenate(end, axis=1)[:rows]
    for k in range(3):
        coarse_coefs_ref[k] = coarse_coefs[k][0]


def natural_kernel(correction_ref, end_ref, correction_out_ref, end_out_ref):
    for source, target in ((correction_ref, correction_out_ref), (end_ref, end_out_ref)):
        for k in range(2):
            target[0, k] = joined(*halves(source[k]))


def hand_kernel(
    arrived_ref,
    coarse_coefs_ref,
    coarse_correction_ref,
    correction_ref,
    end_ref,
    out_ref,
    *coarse_out_ref,
    taker,
):
    rows = correction_ref.shape[2]
    coarse = advance(
        *((arrived_ref[k],) for k in range(2)), *((coarse_coefs_ref[k],) for k in range(3)), COARSE
    )
    takes = lax.axis_index("tm") == taker
    for k in range(2):
        handed = coarse[k][0][:rows]
        out_ref[0, k] = jnp.where(
            takes, joined(handed, handed) + correction_ref[0, k], end_ref[0, k]
        )
        for ref in coarse_out_ref:
            ref[k] = handed + coarse_correction_ref[k]


def edges_kernel(strip_ref, out_ref):
    for k in range(strip_ref.shape[0]):
        out_ref[k] = edge_tile(strip_ref[k])


def widen_kernel(strip_ref, after_ref, before_ref, out_ref, *, swapped):
    for k in range(strip_ref.shape[0]):
        edge = halo(after_ref[k], before_ref[k], swapped)
        out_ref[k] = jnp.concatenate([strip_ref[k], edge], axis=0)


def local_call(kernel, outs, arrays, tables=(), space=pltpu.VMEM, scratch=()):
    vmem, smem = pl.BlockSpec(memory_space=pltpu.VMEM), pl.BlockSpec(memory_space=pltpu.SMEM)
    return pl.pallas_call(
        kernel,
        out_shape=[jax.ShapeDtypeStruct(shape, jnp.float32) for shape in outs],
        in_specs=[pl.BlockSpec(memory_space=space)] * len(arrays) + [smem] * len(tables),
        out_specs=[vmem] * len(outs),
        scratch_shapes=scratch,
        compiler_params=pltpu.CompilerParams(vmem_limit_bytes=4 * 2**20),
    )(*arrays, *tables)


def both_neighbours(tile):
    count = lax.axis_size("space")
    ring = [(i, (i + 1) % count) for i in range(count)]
    if count % 2:
        return (
            lax.ppermute(tile, "space", [(j, i) for i, j in ring]),
            lax.ppermute(tile, "space", ring),
            False,
        )
    swaps = [[pair for i, j in ring[start::2] for pair in ((i, j), (j, i))] for start in (0, 1)]
    outer = lax.ppermute(tile, "space", swaps[1])
    inner = lax.ppermute(tile, "space", swaps[0])
    return inner, outer, True


def from_behind(array):
    count = lax.axis_size("tm")
    return lax.ppermute(array, "tm", [(i, i + 1) for i in range(count - 1)])


def on_device(slice_starts, habitat, capacity_table, prey_motility, predator_motility):
    _, fields, rows, columns = slice_starts.shape
    wide, half = rows + TILE, columns // 2
    slices = lax.axis_size("tm")
    edges, strip = local_call(
        load_kernel,
        [(3, TILE, columns), (3, rows, columns)],
        [pltpu.with_memory_space_constraint(a, pltpu.HBM) for a in (slice_starts, habitat)],
        space=pltpu.HBM,
        scratch=[
            pltpu.VMEM(slice_starts.shape, slice_starts.dtype),
            pltpu.VMEM(habitat.shape, habitat.dtype),
            pltpu.SemaphoreType.DMA((2,)),
        ],
    )
    after, before, swapped = both_neighbours(edges)
    prepared = local_call(
        prepare_kernel,
        [(fields, rows, columns), (4, rows, columns), (4, TILE, half)],
        [strip],
        [prey_motility, predator_motility, capacity_table],
    )
    coarse_end, coarse_coefs, coarse_correction, correction, end = local_call(
        functools.partial(propagate_kernel, swapped=swapped),
        [
            (fields, wide, half),
            (3, wide, half),
            (fields, rows, half),
            (fields, rows, columns),
            (fields, rows, columns),
        ],
        [*prepared, after, before],
    )
    correction, end = local_call(
        natural_kernel, [slice_starts.shape, slice_starts.shape], [correction, end]
    )
    for taker in range(1, slices):
        arrived = from_behind(coarse_end)
        if taker > 1:
            (edges,) = local_call(edges_kernel, [(fields, TILE, half)], [arrived])
            after, before, swapped = both_neighbours(edges)
            (arrived,) = local_call(
                functools.partial(widen_kernel, swapped=swapped),
                [(fields, wide, half)],
                [arrived, after, before],
            )
        last = taker + 1 == slices
        end, *passed = local_call(
            functools.partial(hand_kernel, taker=taker),
            [slice_starts.shape] + [(fields, rows, half)] * (not last),
            [arrived, coarse_coefs, coarse_correction, correction, end],
        )
        coarse_end = None if last else passed[0]
    return end


def solution(mesh):
    placed = (P("tm", None, "space", None), P("space", None), P(), P(), P())
    return jax.shard_map(
        on_device,
        mesh=mesh,
        in_specs=placed,
        out_specs=P("tm", None, "space", None),
        check_vma=False,
    )
```

time: 16.8 us -> 14.7 us (0.87)
  waiting for transfers between devices: 4.9 us -> 2.15 us
  local copies, waits for them, and re-layouts: 1.49 us -> 0.02 us
  starting transfers between devices: 8.07 us -> 9.4 us
  Pallas kernels: 2.04 us -> 2.87 us
    ppermute x1, starting transfers between devices: 3.18 us -> 5.51 us  [both_neighbours(): outer = lax.ppermute(tile, 'space', swaps[1])]
    ppermute x1, waiting for transfers between devices: 3.01 us -> 0.77 us  [both_neighbours(): outer = lax.ppermute(tile, 'space', swaps[1])]
    unnamed x10 -> x6, local copies, waits for them, and re-layouts: 1.49 us -> 0.02 us
    ppermute x1, starting transfers between devices: 4.89 us -> 3.88 us  [from_behind(): return lax.ppermute(array, 'tm', [(i, i + 1) for i in range(count - 1)])]
    pallas_call x2 -> x5, Pallas kernels: 2.04 us -> 2.87 us  [local_call(): pl.pallas_call(kernel, out_shape=[jax.ShapeDtypeStruct(shape, jnp.float32...]
    ppermute x1, waiting for transfers between devices: 1.89 us -> 1.37 us  [from_behind(): return lax.ppermute(array, 'tm', [(i, i + 1) for i in range(count - 1)])]
  transfers between devices with their start and end apart: 3 -> 3, of which waited for: 2 -> 2; matrix products, arithmetic and copies ran while one was open for 0% -> 0% of each run, Pallas kernels for 0% -> 6%
where the time goes in v2:
time: 14.7 us; the launch traced here: 14.5 us
  starting transfers between devices  9.4 us (64%)
  Pallas kernels  2.87 us (20%)
  waiting for transfers between devices  2.15 us (15%)
    ppermute x1, starting transfers between devices, both_neighbours(): outer = lax.ppermute(tile, 'space', swaps[1])  5.51 us
    ppermute x1, starting transfers between devices, from_behind(): return lax.ppermute(array, 'tm', [(i, i + 1) for i in range(count - 1)])  3.88 us
    pallas_call x5, Pallas kernels, local_call(): pl.pallas_call(kernel, out_shape=[jax.ShapeDtypeStruct(shape, jnp.float32...  2.87 us
    ppermute x1, waiting for transfers between devices, from_behind(): return lax.ppermute(array, 'tm', [(i, i + 1) for i in range(count - 1)])  1.37 us
    ppermute x1, waiting for transfers between devices, both_neighbours(): outer = lax.ppermute(tile, 'space', swaps[1])  0.77 us
  transfers between devices with their start and end apart: 3, of which 2 were waited for; matrix products, arithmetic and copies ran while one was open for 0% of the time, Pallas kernels for 6%

profile of v2, /device:TPU:0, one launch (start us, length us, event | category | flops | bytes accessed | tf_op | source)
XLA Modules:
  0.0 14.5 jit_solution(3789824078368701687)
XLA Ops:
  0.0 0.9 %shard_map.55 = (f32[3,8,256]{2,1,0:T(8,128)S(1)}, f32[3,16,256]{2,1,0:T(8,128)S(1)}) custom-call(f32[1,2,16,256]{3,2,1,0:T(8,128)} %starts_hbm.1, s32[16,256]{1,0:T(8,128)} %habitat_hbm.1), custom_call_target="tpu_custom_call" | custom-call | tf_op jit(solution)/shard_map/pallas_call | solution.py:274
  0.9 0.0 copy-start
  0.9 0.0 copy-start.1
  0.9 0.0 copy-start.2
  0.9 5.5 %collective-permute-start.1 = (f32[3,8,256]{2,1,0:T(8,128)S(1)}, f32[3,8,256]{2,1,0:T(8,128)S(1)}, u32[]{:S(2)}, u32[]{:S(2)}) collective-permute-start(f32[3,8,256]{2,1,0:T(8,128)S(1)} %get-tuple-element.21), channel_id=1, source_target_pairs={{1,2},{2,1},{3,4},{4,3},{5,6},{6,5},{7,8},{8,7},{9,10},{10,9},{11,... | collective-permute-start | bytes 73736 | tf_op jit(solution)/shard_map/ppermute | solution.py:294
  6.4 0.0 collective-permute-start
  6.4 0.0 copy-done
  6.4 0.0 copy-done.1
  6.4 0.0 copy-done.2
  6.4 0.7 %shard_map.56 = (f32[2,16,256]{2,1,0:T(8,128)S(1)}, f32[4,16,256]{2,1,0:T(8,128)S(1)}, f32[4,8,128]{2,1,0:T(8,128)S(1)}) custom-call(f32[3,16,256]{2,1,0:T(8,128)S(1)} %get-tuple-element.17.strip_ref, f32[8]{0:T(128)S(1)} %copy-done, f32[8]{0:T(128)S(1)} %copy-done.1, f32[8]{0:T(128)S(1)} %copy-done.2), custom_call_target="tpu_custom_call" | custom-call | tf_op jit(solution)/shard_map/pallas_call | solution.py:274
  7.2 0.8 %collective-permute-done.1.before_ref = f32[3,8,256]{2,1,0:T(8,128)S(1)} collective-permute-done((f32[3,8,256]{2,1,0:T(8,128)S(1)}, f32[3,8,256]{2,1,0:T(8,128)S(1)}, u32[]{:S(2)}, u32[]{:S(2)}) %collective-permute-start.1) | collective-permute-done | bytes 24608 | tf_op jit(solution)/shard_map/ppermute | solution.py:294
  7.9 0.0 collective-permute-done.after_ref
  8.0 0.3 %shard_map.57 = (f32[2,24,128]{2,1,0:T(8,128)S(1)}, f32[3,24,128]{2,1,0:T(8,128)S(1)}, f32[2,16,128]{2,1,0:T(8,128)S(1)}, f32[2,16,256]{2,1,0:T(8,128)S(1)}, f32[2,16,256]{2,1,0:T(8,128)S(1)}) custom-call(f32[2,16,256]{2,1,0:T(8,128)S(1)} %get-tuple-element.18.fields_ref, f32[4,16,256]{2,1,0:T(8,128)S(1)} %get-tuple-element.19.coefs_ref, ...), custom_call_target="tpu_custom_call" | custom-call | tf_op jit(solution)/shard_map/pallas_call | solution.py:274
  8.3 3.9 %collective-permute-start.2 = (f32[2,24,128]{2,1,0:T(8,128)S(1)}, f32[2,24,128]{2,1,0:T(8,128)S(1)}, u32[]{:S(2)}, u32[]{:S(2)}) collective-permute-start(f32[2,24,128]{2,1,0:T(8,128)S(1)} %get-tuple-element.22), channel_id=1, source_target_pairs={{0,16},{1,17},{2,18},{3,19},{4,20},{5,21},{6,22},{7,23},{8,24},{9,... | collective-permute-start | bytes 73736 | tf_op jit(solution)/shard_map/ppermute | solution.py:301
  12.2 0.1 shard_map.58
  12.3 1.4 %collective-permute-done.2.arrived_ref = f32[2,24,128]{2,1,0:T(8,128)S(1)} collective-permute-done((f32[2,24,128]{2,1,0:T(8,128)S(1)}, f32[2,24,128]{2,1,0:T(8,128)S(1)}, u32[]{:S(2)}, u32[]{:S(2)}) %collective-permute-start.2) | collective-permute-done | bytes 24608 | tf_op jit(solution)/shard_map/ppermute | solution.py:301
  13.7 0.8 %shard_map.59 = f32[1,2,16,256]{3,2,1,0:T(8,128)} custom-call(f32[2,24,128]{2,1,0:T(8,128)S(1)} %collective-permute-done.2.arrived_ref, f32[3,24,128]{2,1,0:T(8,128)S(1)} %get-tuple-element.23.coarse_coefs_ref, f32[2,16,128]{2,1,0:T(8,128)S(1)} %get-tuple-element.24.coarse_correction_ref, f32[1,2,16,256]{3,2,1,0:T(8,128)S(1)} %get-tuple-element.27.correction_ref, ...), custom_call_target="tpu_custom_call" | custom-call | tf_op jit(solution)/shard_map/pallas_call | solution.py:274
Async XLA Ops:
  0.9 5.6 %copy-start = (f32[8]{0:T(128)S(1)}, f32[8]{0:T(128)}, u32[]{:S(2)}) copy-start(f32[8]{0:T(128)} %prey_ref.1) | copy-start | bytes 100
  0.9 5.5 %copy-start.1 = (f32[8]{0:T(128)S(1)}, f32[8]{0:T(128)}, u32[]{:S(2)}) copy-start(f32[8]{0:T(128)} %pred_ref.1) | copy-start | bytes 100
  0.9 5.5 %copy-start.2 = (f32[8]{0:T(128)S(1)}, f32[8]{0:T(128)}, u32[]{:S(2)}) copy-start(f32[8]{0:T(128)} %cap_ref.1) | copy-start | bytes 100
  0.9 7.0 %collective-permute-start.1 = (f32[3,8,256]{2,1,0:T(8,128)S(1)}, f32[3,8,256]{2,1,0:T(8,128)S(1)}, u32[]{:S(2)}, u32[]{:S(2)}) collective-permute-start(f32[3,8,256]{2,1,0:T(8,128)S(1)} %get-tuple-element.21), channel_id=1, source_target_pairs={{1,2},{2,1},{3,4},{4,3},{5,6},{6,5},{7,8},{8,7},{9,10},{10,9},{11,... | collective-permute-start | bytes 73736 | tf_op jit(solution)/shard_map/ppermute | solution.py:294
  6.4 1.5 %collective-permute-start = (f32[3,8,256]{2,1,0:T(8,128)S(1)}, f32[3,8,256]{2,1,0:T(8,128)S(1)}, u32[]{:S(2)}, u32[]{:S(2)}) collective-permute-start(f32[3,8,256]{2,1,0:T(8,128)S(1)} %get-tuple-element.21), channel_id=1, source_target_pairs={{0,1},{1,0},{2,3},{3,2},{4,5},{5,4},{6,7},{7,6},{8,9},{9,8},{10,11... | collective-permute-start | bytes 73736 | tf_op jit(solution)/shard_map/ppermute | solution.py:295
  8.3 5.4 %collective-permute-start.2 = (f32[2,24,128]{2,1,0:T(8,128)S(1)}, f32[2,24,128]{2,1,0:T(8,128)S(1)}, u32[]{:S(2)}, u32[]{:S(2)}) collective-permute-start(f32[2,24,128]{2,1,0:T(8,128)S(1)} %get-tuple-element.22), channel_id=1, source_target_pairs={{0,16},{1,17},{2,18},{3,19},{4,20},{5,21},{6,22},{7,23},{8,24},{9,... | collective-permute-start | bytes 73736 | tf_op jit(solution)/shard_map/ppermute | solution.py:301

commit v3 on v2

--- a/solution.py
+++ b/solution.py
@@ -298,7 +298,7 @@
 
 def from_behind(array):
     count = lax.axis_size("tm")
-    return lax.ppermute(array, "tm", [(i, i + 1) for i in range(count - 1)])
+    return lax.ppermute(array, "tm", [(i, (i + 1) % count) for i in range(count)])
 
 
 def on_device(slice_starts, habitat, capacity_table, prey_motility, predator_motility):

time: 14.7 us -> 13.2 us (0.90)
  starting transfers between devices: 9.4 us -> 7.56 us
  waiting for transfers between devices: 2.15 us -> 2.49 us
    ppermute x1, starting transfers between devices: 3.88 us -> 2.04 us  [from_behind(): lax.ppermute(array, 'tm', [(i, (i + 1) % count) for i in range(count)])]
    ppermute x1, waiting for transfers between devices: 1.37 us -> 1.72 us  [from_behind(): lax.ppermute(array, 'tm', [(i, (i + 1) % count) for i in range(count)])]
  transfers between devices with their start and end apart: 3 -> 3, of which waited for: 2 -> 2; matrix products, arithmetic and copies ran while one was open for 0% -> 0% of each run, Pallas kernels for 6% -> 7%
where the time goes in v3:
time: 13.2 us; the launch traced here: 13 us
  starting transfers between devices  7.56 us (57%)
  Pallas kernels  2.87 us (22%)
  waiting for transfers between devices  2.49 us (19%)
    ppermute x1, starting transfers between devices, both_neighbours(): outer = lax.ppermute(tile, 'space', swaps[1])  5.51 us
    pallas_call x5, Pallas kernels, local_call(): pl.pallas_call(kernel, out_shape=[jax.ShapeDtypeStruct(shape, jnp.float32...  2.87 us
    ppermute x1, starting transfers between devices, from_behind(): lax.ppermute(array, 'tm', [(i, (i + 1) % count) for i in range(count)])  2.04 us
    ppermute x1, waiting for transfers between devices, from_behind(): lax.ppermute(array, 'tm', [(i, (i + 1) % count) for i in range(count)])  1.72 us
    ppermute x1, waiting for transfers between devices, both_neighbours(): outer = lax.ppermute(tile, 'space', swaps[1])  0.77 us
  transfers between devices with their start and end apart: 3, of which 2 were waited for; matrix products, arithmetic and copies ran while one was open for 0% of the time, Pallas kernels for 7%

profile of v3, /device:TPU:0, one launch (start us, length us, event | category | flops | bytes accessed | tf_op | source)
XLA Modules:
  0.0 13.0 jit_solution(18067748809731890019)
XLA Ops:
  0.0 0.9 %shard_map.55 = (f32[3,8,256]{2,1,0:T(8,128)S(1)}, f32[3,16,256]{2,1,0:T(8,128)S(1)}) custom-call(f32[1,2,16,256]{3,2,1,0:T(8,128)} %starts_hbm.1, s32[16,256]{1,0:T(8,128)} %habitat_hbm.1), custom_call_target="tpu_custom_call" | custom-call | tf_op jit(solution)/shard_map/pallas_call | solution.py:274
  0.9 0.0 copy-start
  0.9 0.0 copy-start.1
  0.9 0.0 copy-start.2
  0.9 5.5 %collective-permute-start.1 = (f32[3,8,256]{2,1,0:T(8,128)S(1)}, f32[3,8,256]{2,1,0:T(8,128)S(1)}, u32[]{:S(2)}, u32[]{:S(2)}) collective-permute-start(f32[3,8,256]{2,1,0:T(8,128)S(1)} %get-tuple-element.21), channel_id=1, source_target_pairs={{1,2},{2,1},{3,4},{4,3},{5,6},{6,5},{7,8},{8,7},{9,10},{10,9},{11,... | collective-permute-start | bytes 73736 | tf_op jit(solution)/shard_map/ppermute | solution.py:294
  6.4 0.0 collective-permute-start
  6.4 0.0 copy-done
  6.4 0.0 copy-done.1
  6.4 0.0 copy-done.2
  6.4 0.7 %shard_map.56 = (f32[2,16,256]{2,1,0:T(8,128)S(1)}, f32[4,16,256]{2,1,0:T(8,128)S(1)}, f32[4,8,128]{2,1,0:T(8,128)S(1)}) custom-call(f32[3,16,256]{2,1,0:T(8,128)S(1)} %get-tuple-element.17.strip_ref, f32[8]{0:T(128)S(1)} %copy-done, f32[8]{0:T(128)S(1)} %copy-done.1, f32[8]{0:T(128)S(1)} %copy-done.2), custom_call_target="tpu_custom_call" | custom-call | tf_op jit(solution)/shard_map/pallas_call | solution.py:274
  7.2 0.8 %collective-permute-done.1.before_ref = f32[3,8,256]{2,1,0:T(8,128)S(1)} collective-permute-done((f32[3,8,256]{2,1,0:T(8,128)S(1)}, f32[3,8,256]{2,1,0:T(8,128)S(1)}, u32[]{:S(2)}, u32[]{:S(2)}) %collective-permute-start.1) | collective-permute-done | bytes 24608 | tf_op jit(solution)/shard_map/ppermute | solution.py:294
  7.9 0.0 collective-permute-done.after_ref
  8.0 0.3 %shard_map.57 = (f32[2,24,128]{2,1,0:T(8,128)S(1)}, f32[3,24,128]{2,1,0:T(8,128)S(1)}, f32[2,16,128]{2,1,0:T(8,128)S(1)}, f32[2,16,256]{2,1,0:T(8,128)S(1)}, f32[2,16,256]{2,1,0:T(8,128)S(1)}) custom-call(f32[2,16,256]{2,1,0:T(8,128)S(1)} %get-tuple-element.18.fields_ref, f32[4,16,256]{2,1,0:T(8,128)S(1)} %get-tuple-element.19.coefs_ref, ...), custom_call_target="tpu_custom_call" | custom-call | tf_op jit(solution)/shard_map/pallas_call | solution.py:274
  8.3 2.0 %collective-permute-start.2 = (f32[2,24,128]{2,1,0:T(8,128)S(1)}, f32[2,24,128]{2,1,0:T(8,128)S(1)}, u32[]{:S(2)}, u32[]{:S(2)}) collective-permute-start(f32[2,24,128]{2,1,0:T(8,128)S(1)} %get-tuple-element.22), channel_id=1, source_target_pairs={{0,16},{16,0},{1,17},{17,1},{2,18},{18,2},{3,19},{19,3},{4,20},{20... | collective-permute-start | bytes 73736 | tf_op jit(solution)/shard_map/ppermute | solution.py:301
  10.3 0.1 shard_map.58
  10.4 1.7 %collective-permute-done.2.arrived_ref = f32[2,24,128]{2,1,0:T(8,128)S(1)} collective-permute-done((f32[2,24,128]{2,1,0:T(8,128)S(1)}, f32[2,24,128]{2,1,0:T(8,128)S(1)}, u32[]{:S(2)}, u32[]{:S(2)}) %collective-permute-start.2) | collective-permute-done | bytes 24608 | tf_op jit(solution)/shard_map/ppermute | solution.py:301
  12.2 0.8 %shard_map.59 = f32[1,2,16,256]{3,2,1,0:T(8,128)} custom-call(f32[2,24,128]{2,1,0:T(8,128)S(1)} %collective-permute-done.2.arrived_ref, f32[3,24,128]{2,1,0:T(8,128)S(1)} %get-tuple-element.23.coarse_coefs_ref, f32[2,16,128]{2,1,0:T(8,128)S(1)} %get-tuple-element.24.coarse_correction_ref, f32[1,2,16,256]{3,2,1,0:T(8,128)S(1)} %get-tuple-element.27.correction_ref, ...), custom_call_target="tpu_custom_call" | custom-call | tf_op jit(solution)/shard_map/pallas_call | solution.py:274
Async XLA Ops:
  0.9 5.6 %copy-start = (f32[8]{0:T(128)S(1)}, f32[8]{0:T(128)}, u32[]{:S(2)}) copy-start(f32[8]{0:T(128)} %prey_ref.1) | copy-start | bytes 100
  0.9 5.5 %copy-start.1 = (f32[8]{0:T(128)S(1)}, f32[8]{0:T(128)}, u32[]{:S(2)}) copy-start(f32[8]{0:T(128)} %pred_ref.1) | copy-start | bytes 100
  0.9 5.5 %copy-start.2 = (f32[8]{0:T(128)S(1)}, f32[8]{0:T(128)}, u32[]{:S(2)}) copy-start(f32[8]{0:T(128)} %cap_ref.1) | copy-start | bytes 100
  0.9 7.0 %collective-permute-start.1 = (f32[3,8,256]{2,1,0:T(8,128)S(1)}, f32[3,8,256]{2,1,0:T(8,128)S(1)}, u32[]{:S(2)}, u32[]{:S(2)}) collective-permute-start(f32[3,8,256]{2,1,0:T(8,128)S(1)} %get-tuple-element.21), channel_id=1, source_target_pairs={{1,2},{2,1},{3,4},{4,3},{5,6},{6,5},{7,8},{8,7},{9,10},{10,9},{11,... | collective-permute-start | bytes 73736 | tf_op jit(solution)/shard_map/ppermute | solution.py:294
  6.4 1.5 %collective-permute-start = (f32[3,8,256]{2,1,0:T(8,128)S(1)}, f32[3,8,256]{2,1,0:T(8,128)S(1)}, u32[]{:S(2)}, u32[]{:S(2)}) collective-permute-start(f32[3,8,256]{2,1,0:T(8,128)S(1)} %get-tuple-element.21), channel_id=1, source_target_pairs={{0,1},{1,0},{2,3},{3,2},{4,5},{5,4},{6,7},{7,6},{8,9},{9,8},{10,11... | collective-permute-start | bytes 73736 | tf_op jit(solution)/shard_map/ppermute | solution.py:295
  8.3 3.9 %collective-permute-start.2 = (f32[2,24,128]{2,1,0:T(8,128)S(1)}, f32[2,24,128]{2,1,0:T(8,128)S(1)}, u32[]{:S(2)}, u32[]{:S(2)}) collective-permute-start(f32[2,24,128]{2,1,0:T(8,128)S(1)} %get-tuple-element.22), channel_id=1, source_target_pairs={{0,16},{16,0},{1,17},{17,1},{2,18},{18,2},{3,19},{19,3},{4,20},{20... | collective-permute-start | bytes 73736 | tf_op jit(solution)/shard_map/ppermute | solution.py:301
